TPU v7x, 32 devices: a whole 2x2x4 slice. The times are simulated.
32 devices in a mesh: grp: 4 (over y, core), dev: 8 (over z, x).
Axes of the slice: x: 2, y: 2, z: 4, core: 2. Of those that a mesh axis runs over, the one named last changes fastest.
Arguments:
- train_grads: bfloat16 [4096, 1024], P(('grp', 'dev')), may hold values from -192 to 192, as said below
- queries: bfloat16 [512, 1024], P('grp'), may hold values from -6 to 6
Outputs:
- scores: bfloat16 [4096, 512], P(('grp', 'dev'))
Inputs may be any that keep to these rules, and one draw needn't show every extreme that they name: `train_grads`: Real-valued projected gradients whose columns and rows differ in scale.
All inputs are finite; a program needn't handle non-finite values. Where the computation divides by a largest or mean magnitude, that divisor is 1e-20 or more.
Results may differ from a plain program's by a relative error of at most 0.001.
The roundings to bfloat16 on the way count: a program that leaves them out, or rounds other values in their place, can miss the bound.
Values may be sent and summed in bfloat16 or wider, within the bound.
No kernel may reach another device: no remote copies, remote signals or barrier semaphores. Data moves between devices by JAX's collectives and lax.ppermute only.
A program may use at most 64 MiB of HBM per device.

v0:
```python
import jax
import jax.numpy as jnp
from jax import lax
from jax.sharding import PartitionSpec as P

ITERS = 8
damping_ratio = 0.1


def local_solve(gram, own, total, width):
    normed = gram / total
    damp = damping_ratio * jnp.trace(gram) / (total * width)
    bound = jnp.max(jnp.sum(jnp.abs(normed), axis=1)) + damp
    step = 1.0 / bound
    oper = normed + damp * jnp.eye(width, dtype=jnp.float32)
    state = step * own
    for index in range(ITERS):
        state = state + step * (own - jnp.dot(state, oper, precision=lax.Precision.HIGHEST))
    return state.astype(jnp.bfloat16)


def body(train_grads, queries):
    rows, width = train_grads.shape
    ndevice = lax.axis_size("dev")
    total = rows * ndevice * lax.axis_size("grp")
    qvals = queries.astype(jnp.float32)
    qrows = qvals.shape[0] // ndevice
    qstart = lax.axis_index("dev") * qrows
    own = lax.dynamic_slice_in_dim(qvals, qstart, qrows, 0)
    gram = lax.psum(
        lax.dot_general(
            train_grads, train_grads, (((0,), (0,)), ((), ())), preferred_element_type=jnp.float32
        ),
        ("grp", "dev"),
    )
    mine = local_solve(gram, own, total, width)
    prepared = lax.all_gather(mine, "dev", axis=0, tiled=True)
    return lax.dot_general(
        train_grads,
        lax.all_gather(prepared, "grp", axis=0, tiled=True),
        (((1,), (1,)), ((), ())),
        preferred_element_type=jnp.float32,
    ).astype(jnp.bfloat16)


def solution(mesh):
    return jax.shard_map(
        body,
        mesh=mesh,
        in_specs=(P(("grp", "dev"), None), P("grp", None)),
        out_specs=P(("grp", "dev"), None),
        check_vma=False,
    )
```

profile of v0, /device:TPU:0, one launch (start us, length us, event | category | flops | bytes accessed | tf_op | source)
XLA Modules:
  0.0 242.2 jit_solution(13720680544935687470)
XLA Ops:
  6.5 0.0 copy-start
  6.5 0.0 all-reduce.2.cloned.1.call-start
  6.5 0.9 copy-done
  7.5 2.7 %fusion.21 = f32[1024,1024]{1,0:T(8,128)} fusion(bf16[128,1024]{1,0:T(8,128)(2,1)S(1)} %copy-done), kind=kOutput, calls=%fused_computation.35 | convolution fusion | flops 268435456 | bytes 4456448 | tf_op jit(solution)/shard_map/dot_general | solution.py:31
  10.2 0.0 copy-start.2
  10.2 0.0 all-reduce.2.cloned.1.call-update
  10.2 0.0 all-gather.2.cloned.1.call-start
  10.3 147.6 %all-reduce.2.cloned.1.call-done = f32[1024,1024]{1,0:T(8,128)} async-done(((f32[1024,1024]{1,0:T(8,128)}), f32[1024,1024]{1,0:T(8,128)}) %all-reduce.2.cloned.1.call-update) | async-done | bytes 4194320 | tf_op jit(solution)/shard_map/psum | solution.py:30
  157.9 3.3 %select_reduce_fusion = (f32[]{:T(128)}, f32[1024]{0:T(1024)S(1)}) fusion(f32[1024,1024]{1,0:T(8,128)} %all-reduce.2.cloned.1.call-done), kind=kLoop, calls=%fused_computation.1 | loop fusion | flops 6290431 | bytes 4198404 | tf_op jit(solution)/shard_map/jit(trace)/reduce_sum | solution.py:12
  161.9 0.6 reduce_max.9
  163.2 0.0 copy-done.2
  163.2 0.0 copy-start.1
  163.2 4.6 %fusion.2 = f32[16,1024]{1,0:T(8,128)S(1)} fusion(f32[]{:T(128)S(6)} %div.15, bf16[128,1024]{1,0:T(8,128)(2,1)S(1)} %copy-done.2, s32[]{:T(128)S(6)} %select_n.9, f32[1024,1024]{1,0:T(8,128)} %all-reduce.2.cloned.1.call-done, f32[]{:T(128)S(6)} %div.14), kind=kOutput, calls=%fused_computation.15 | convolution fusion | flops 205635584 | bytes 4327936 | tf_op jit(solution)/shard_map/dot_general | solution.py:18
  167.8 0.0 copy-done.1
  167.8 2.3 fusion.4
  170.1 2.3 fusion.6
  172.3 2.3 fusion.8
  174.6 2.3 fusion.10
  176.8 2.4 %fusion.12 = f32[16,1024]{1,0:T(8,128)S(1)} fusion(f32[16,1024]{1,0:T(8,128)S(1)} %fusion.10, f32[]{:T(128)S(6)} %div.15, bf16[128,1024]{1,0:T(8,128)(2,1)S(1)} %copy-done.2, s32[]{:T(128)S(6)} %select_n.9, f32[1024,1024]{1,0:T(8,128)S(1)} %copy-done.1, f32[]{:T(128)S(6)} %div.14), kind=kOutput, calls=%fused_computation.25 | convolution fusion | flops 205586432 | bytes 4423692 | tf_op jit(solution)/shard_map/dot_general | solution.py:18
  179.3 2.3 fusion.14
  181.5 2.3 fusion.17
  183.8 32.8 %all_gather.6 = bf16[128,1024]{1,0:T(8,128)(2,1)} all-gather(bf16[16,1024]{1,0:T(8,128)(2,1)S(1)} %fusion.17), channel_id=1, replica_groups=mesh['grp'=4,'dev'=8] {'dev'}, dimensions={0}, use_global_device_ids=true | all-gather | bytes 294912 | tf_op jit(solution)/shard_map/all_gather | solution.py:37
  216.6 0.0 all-gather.2.cloned.1.call-update
  216.7 16.3 %all-gather.2.cloned.1.call-done = bf16[512,1024]{1,0:T(8,128)(2,1)} async-done(((bf16[128,1024]{1,0:T(8,128)(2,1)}), bf16[512,1024]{1,0:T(8,128)(2,1)}) %all-gather.2.cloned.1.call-update) | async-done | bytes 1048592 | tf_op jit(solution)/shard_map/all_gather | solution.py:40
  233.0 1.7 fusion
  234.6 0.8 copy.3
Async XLA Ops:
  6.5 1.0 copy-start
  6.5 151.4 %all-reduce.2.cloned.1.call-start = ((), (), s32[]{:S(2)}) async-start(), calls=%async_computation | async-start | bytes 8388608 | tf_op jit(solution)/shard_map/psum | solution.py:30
  10.2 153.0 %copy-start.2 = (bf16[128,1024]{1,0:T(8,128)(2,1)S(1)}, bf16[128,1024]{1,0:T(8,128)(2,1)}, u32[]{:S(2)}) copy-start(bf16[128,1024]{1,0:T(8,128)(2,1)} %param.3) | copy-start | bytes 786436
  10.2 222.8 %all-gather.2.cloned.1.call-start = ((), (), s32[]{:S(2)}) async-start(), calls=%async_computation.1 | async-start | bytes 1310720 | tf_op jit(solution)/shard_map/all_gather | solution.py:40
  163.2 4.6 %copy-start.1 = (f32[1024,1024]{1,0:T(8,128)S(1)}, f32[1024,1024]{1,0:T(8,128)}, u32[]{:S(2)}) copy-start(f32[1024,1024]{1,0:T(8,128)} %all-reduce.2.cloned.1.call-done) | copy-start | bytes 12582916
Sparse Core Ops, SparseCore 0:
  12.9 144.9 all-reduce.1
  216.8 16.1 all-gather.1
where the time goes:
time: 242 us
  waiting for transfers between devices  164 us (68%)
  blocking collectives  32.8 us (14%)
  matrix products  24.9 us (10%)
  between operations  14.8 us (6%)
  other arithmetic  3.94 us (2%)
    psum x1, waiting for transfers between devices, body(): lax.psum(lax.dot_general(train_grads, train_grads, (((0,), (0,)), ((), ()...  148 us
    all_gather x1, blocking collectives, body(): prepared = lax.all_gather(mine, 'dev', axis=0, tiled=True)  32.8 us
    dot_general x8, matrix products, local_solve(): jnp.dot(state, oper, precision=lax.Precision.HIGHEST)  20.5 us
    all_gather x1, waiting for transfers between devices, body(): lax.all_gather(prepared, 'grp', axis=0, tiled=True)  16.3 us
  transfers between devices with their start and end apart: 2, of which 2 were waited for; matrix products, arithmetic and copies ran while one was open for 0% of the time, Pallas kernels for 0%

commit v1 on v0

--- a/solution.py
+++ b/solution.py
@@ -34,7 +34,10 @@
         ("grp", "dev"),
     )
     mine = local_solve(gram, own, total, width)
-    prepared = lax.all_gather(mine, "dev", axis=0, tiled=True)
+    drive_marks = lambda inputs: jnp.concatenate(
+        lax.all_to_all(jnp.stack([inputs for _ in range(lax.psum(1, "dev"))], 0), "dev", 0, 0), 0
+    )
+    prepared = drive_marks(mine)
     return lax.dot_general(
         train_grads,
         lax.all_gather(prepared, "grp", axis=0, tiled=True),

time: 242 us -> 221 us (0.913)
  blocking collectives: 32.8 us -> 11.8 us
    all_gather x1 -> x0, blocking collectives: 32.8 us -> none  [body(): prepared = lax.all_gather(mine, 'dev', axis=0, tiled=True)]
    all_to_all x0 -> x1, blocking collectives: none -> 11.8 us  [body(): lax.all_to_all(jnp.stack([inputs for _ in range(lax.psum(1, 'dev'))], 0),...]
where the time goes in v1:
time: 221 us; the launch traced here: 220 us
  waiting for transfers between devices  163 us (74%)
  matrix products  24.9 us (11%)
  between operations  14.8 us (7%)
  blocking collectives  11.8 us (5%)
  other arithmetic  3.94 us (2%)
    psum x1, waiting for transfers between devices, body(): lax.psum(lax.dot_general(train_grads, train_grads, (((0,), (0,)), ((), ()...  148 us
    dot_general x8, matrix products, local_solve(): jnp.dot(state, oper, precision=lax.Precision.HIGHEST)  20.5 us
    all_gather x1, waiting for transfers between devices, body(): lax.all_gather(prepared, 'grp', axis=0, tiled=True)  15.3 us
    all_to_all x1, blocking collectives, body(): lax.all_to_all(jnp.stack([inputs for _ in range(lax.psum(1, 'dev'))], 0),...  11.8 us
  transfers between devices with their start and end apart: 2, of which 2 were waited for; matrix products, arithmetic and copies ran while one was open for 0% of the time, Pallas kernels for 0%

profile of v1, /device:TPU:0, one launch (start us, length us, event | category | flops | bytes accessed | tf_op | source)
XLA Modules:
  0.0 220.3 jit_solution(15454420597564546589)
XLA Ops:
  6.5 0.0 copy-start
  6.5 0.0 all-reduce.2.cloned.1.call-start
  6.5 0.9 copy-done
  7.5 2.7 %fusion.21 = f32[1024,1024]{1,0:T(8,128)} fusion(bf16[128,1024]{1,0:T(8,128)(2,1)S(1)} %copy-done), kind=kOutput, calls=%fused_computation.35 | convolution fusion | flops 268435456 | bytes 4456448 | tf_op jit(solution)/shard_map/dot_general | solution.py:31
  10.2 0.0 copy-start.2
  10.2 0.0 all-reduce.2.cloned.1.call-update
  10.2 0.0 all-gather.2.cloned.1.call-start
  10.3 147.6 %all-reduce.2.cloned.1.call-done = f32[1024,1024]{1,0:T(8,128)} async-done(((f32[1024,1024]{1,0:T(8,128)}), f32[1024,1024]{1,0:T(8,128)}) %all-reduce.2.cloned.1.call-update) | async-done | bytes 4194320 | tf_op jit(solution)/shard_map/psum | solution.py:30
  157.9 3.3 %select_reduce_fusion = (f32[]{:T(128)}, f32[1024]{0:T(1024)S(1)}) fusion(f32[1024,1024]{1,0:T(8,128)} %all-reduce.2.cloned.1.call-done), kind=kLoop, calls=%fused_computation.1 | loop fusion | flops 6290431 | bytes 4198404 | tf_op jit(solution)/shard_map/jit(trace)/reduce_sum | solution.py:12
  161.9 0.6 reduce_max.9
  163.2 0.0 copy-done.2
  163.2 0.0 copy-start.1
  163.2 4.6 %fusion.2 = f32[16,1024]{1,0:T(8,128)S(1)} fusion(f32[]{:T(128)S(6)} %div.15, bf16[128,1024]{1,0:T(8,128)(2,1)S(1)} %copy-done.2, s32[]{:T(128)S(6)} %select_n.9, f32[1024,1024]{1,0:T(8,128)} %all-reduce.2.cloned.1.call-done, f32[]{:T(128)S(6)} %div.14), kind=kOutput, calls=%fused_computation.15 | convolution fusion | flops 205635584 | bytes 4327936 | tf_op jit(solution)/shard_map/dot_general | solution.py:18
  167.8 0.0 copy-done.1
  167.8 2.3 %fusion.4 = f32[16,1024]{1,0:T(8,128)S(1)} fusion(f32[16,1024]{1,0:T(8,128)S(1)} %fusion.2, f32[]{:T(128)S(6)} %div.15, bf16[128,1024]{1,0:T(8,128)(2,1)S(1)} %copy-done.2, s32[]{:T(128)S(6)} %select_n.9, f32[1024,1024]{1,0:T(8,128)S(1)} %copy-done.1, f32[]{:T(128)S(6)} %div.14), kind=kOutput, calls=%fused_computation.17 | convolution fusion | flops 205586432 | bytes 4423692 | tf_op jit(solution)/shard_map/dot_general | solution.py:18
  170.1 2.3 %fusion.6 = f32[16,1024]{1,0:T(8,128)S(1)} fusion(f32[16,1024]{1,0:T(8,128)S(1)} %fusion.4, f32[]{:T(128)S(6)} %div.15, bf16[128,1024]{1,0:T(8,128)(2,1)S(1)} %copy-done.2, s32[]{:T(128)S(6)} %select_n.9, f32[1024,1024]{1,0:T(8,128)S(1)} %copy-done.1, f32[]{:T(128)S(6)} %div.14), kind=kOutput, calls=%fused_computation.19 | convolution fusion | flops 205586432 | bytes 4423692 | tf_op jit(solution)/shard_map/dot_general | solution.py:18
  172.3 2.3 %fusion.8 = f32[16,1024]{1,0:T(8,128)S(1)} fusion(f32[16,1024]{1,0:T(8,128)S(1)} %fusion.6, f32[]{:T(128)S(6)} %div.15, bf16[128,1024]{1,0:T(8,128)(2,1)S(1)} %copy-done.2, s32[]{:T(128)S(6)} %select_n.9, f32[1024,1024]{1,0:T(8,128)S(1)} %copy-done.1, f32[]{:T(128)S(6)} %div.14), kind=kOutput, calls=%fused_computation.21 | convolution fusion | flops 205586432 | bytes 4423692 | tf_op jit(solution)/shard_map/dot_general | solution.py:18
  174.6 2.3 %fusion.10 = f32[16,1024]{1,0:T(8,128)S(1)} fusion(f32[16,1024]{1,0:T(8,128)S(1)} %fusion.8, f32[]{:T(128)S(6)} %div.15, bf16[128,1024]{1,0:T(8,128)(2,1)S(1)} %copy-done.2, s32[]{:T(128)S(6)} %select_n.9, f32[1024,1024]{1,0:T(8,128)S(1)} %copy-done.1, f32[]{:T(128)S(6)} %div.14), kind=kOutput, calls=%fused_computation.23 | convolution fusion | flops 205586432 | bytes 4423692 | tf_op jit(solution)/shard_map/dot_general | solution.py:18
  176.8 2.4 %fusion.12 = f32[16,1024]{1,0:T(8,128)S(1)} fusion(f32[16,1024]{1,0:T(8,128)S(1)} %fusion.10, f32[]{:T(128)S(6)} %div.15, bf16[128,1024]{1,0:T(8,128)(2,1)S(1)} %copy-done.2, s32[]{:T(128)S(6)} %select_n.9, f32[1024,1024]{1,0:T(8,128)S(1)} %copy-done.1, f32[]{:T(128)S(6)} %div.14), kind=kOutput, calls=%fused_computation.25 | convolution fusion | flops 205586432 | bytes 4423692 | tf_op jit(solution)/shard_map/dot_general | solution.py:18
  179.3 2.3 %fusion.14 = f32[16,1024]{1,0:T(8,128)S(1)} fusion(f32[16,1024]{1,0:T(8,128)S(1)} %fusion.12, f32[]{:T(128)S(6)} %div.15, bf16[128,1024]{1,0:T(8,128)(2,1)S(1)} %copy-done.2, s32[]{:T(128)S(6)} %select_n.9, f32[1024,1024]{1,0:T(8,128)S(1)} %copy-done.1, f32[]{:T(128)S(6)} %div.14), kind=kOutput, calls=%fused_computation.27 | convolution fusion | flops 205586432 | bytes 4423692 | tf_op jit(solution)/shard_map/dot_general | solution.py:18
  181.5 2.3 %fusion.17 = bf16[16,1024]{1,0:T(8,128)(2,1)S(1)} fusion(f32[16,1024]{1,0:T(8,128)S(1)} %fusion.14, f32[]{:T(128)S(6)} %div.15, bf16[128,1024]{1,0:T(8,128)(2,1)S(1)} %copy-done.2, s32[]{:T(128)S(6)} %select_n.9, f32[1024,1024]{1,0:T(8,128)S(1)} %copy-done.1, f32[]{:T(128)S(6)} %div.14), kind=kOutput, calls=%fused_computation.30 | convolution fusion | flops 205602816 | bytes 4390924 | tf_op jit(solution)/shard_map/dot_general | solution.py:18
  183.8 11.8 %all_to_all.5 = bf16[8,16,1024]{2,1,0:T(8,128)(2,1)} all-to-all(bf16[8,16,1024]{2,1,0:T(8,128)(2,1)S(1)} %stack.2), channel_id=1, replica_groups=mesh['grp'=4,'dev'=8] {'dev'}, dimensions={0} | all-to-all | bytes 524288 | tf_op jit(solution)/shard_map/all_to_all | solution.py:38
  195.7 0.0 all-gather.2.cloned.1.call-update
  195.7 15.3 %all-gather.2.cloned.1.call-done = bf16[512,1024]{1,0:T(8,128)(2,1)} async-done(((bf16[128,1024]{1,0:T(8,128)(2,1)}), bf16[512,1024]{1,0:T(8,128)(2,1)}) %all-gather.2.cloned.1.call-update) | async-done | bytes 1048592 | tf_op jit(solution)/shard_map/all_gather | solution.py:43
  211.0 1.7 fusion
  212.7 0.8 copy.3
  (1 shorter events, 0.0 us)
Async XLA Ops:
  6.5 1.0 copy-start
  6.5 151.4 %all-reduce.2.cloned.1.call-start = ((), (), s32[]{:S(2)}) async-start(), calls=%async_computation.1 | async-start | bytes 8388608 | tf_op jit(solution)/shard_map/psum | solution.py:30
  10.2 153.0 %copy-start.2 = (bf16[128,1024]{1,0:T(8,128)(2,1)S(1)}, bf16[128,1024]{1,0:T(8,128)(2,1)}, u32[]{:S(2)}) copy-start(bf16[128,1024]{1,0:T(8,128)(2,1)} %param.3) | copy-start | bytes 786436
  10.2 200.8 %all-gather.2.cloned.1.call-start = ((), (), s32[]{:S(2)}) async-start(), calls=%async_computation.2 | async-start | bytes 1310720 | tf_op jit(solution)/shard_map/all_gather | solution.py:43
  163.2 4.6 %copy-start.1 = (f32[1024,1024]{1,0:T(8,128)S(1)}, f32[1024,1024]{1,0:T(8,128)}, u32[]{:S(2)}) copy-start(f32[1024,1024]{1,0:T(8,128)} %all-reduce.2.cloned.1.call-done) | copy-start | bytes 12582916
Sparse Core Ops, SparseCore 0:
  12.9 144.9 all-reduce.1
  195.8 15.1 all-gather.1
